TPU v7x, 32 devices: a whole 2x2x4 slice. The times are simulated.
32 devices in a mesh: groups: 2 (over y), row: 16 (over z, x, core).
Axes of the slice: x: 2, y: 2, z: 4, core: 2. Of those that a mesh axis runs over, the one named last changes fastest.
Arguments:
- frames_in: bfloat16 [512, 6144], P(('groups', 'row')), parts along dimension 0, may hold values from -6 to 6
- clip_ids: int32 [512], P(('groups', 'row')), parts along dimension 0, may hold values from 0 to 15, as said below
- norm_gain: float32 [6144], replicated, may hold values from 0.1 to 1.9
- expand_weight: bfloat16 [6144, 24576], P(None, 'row'), may hold values from -0.078125 to 0.078125
- reduce_weight: bfloat16 [24576, 6144], P('row'), may hold values from -0.0390625 to 0.0390625
- conn_gain: float32 [6144], replicated, may hold values from 0.1 to 1.9
- conn_weight: bfloat16 [6144, 8192], P(None, 'row'), may hold values from -0.078125 to 0.078125
Outputs:
- visual_tokens: bfloat16 [32, 8192], P(('groups', 'row')), parts along dimension 0
There are 2 independent parts, one for each index of `groups`. A program takes and returns all parts, laid end to end along the dimension named above; an argument that names none is the same for every part. Nothing has to cross between parts.
Inputs may be any that keep to these rules, and one draw needn't show every extreme that they name: `clip_ids`: every clip number is named by exactly 16 frame tokens, which may lie on any devices.
All inputs are finite; a program needn't handle non-finite values.
Results may differ from a plain program's by a relative error of at most 0.0058.
Values may be sent and summed in bfloat16 or wider, within the bound.
A program may use at most 384 MiB of HBM per device.

v0:
```python
import jax
import jax.numpy as jnp
from jax import lax
from jax.sharding import PartitionSpec as P

FRAMES = 16


epsilon = 1e-06


def swapped(shard, axis, distance):
    return lax.ppermute(shard, axis, [(i, i ^ 1 << distance) for i in range(lax.axis_size(axis))])


def layer_norm(values, gain_row):
    average = jnp.mean(values, axis=-1, keepdims=True)
    centered = values - average
    variance = jnp.mean(centered * centered, axis=-1, keepdims=True)
    return centered * lax.rsqrt(variance + epsilon) * gain_row


def clip_onehot(clip_list, clip_count):
    return (clip_list[:, None] == jnp.arange(clip_count, dtype=jnp.int32)[None, :]).astype(
        jnp.bfloat16
    )


def pool_rows(onehot, values):
    return lax.dot_general(
        onehot, values, (((0,), (0,)), ((), ())), preferred_element_type=jnp.float32
    )


def hidden_pool(row_block, clip_list, weight_block, clip_count):
    pre_act = jnp.dot(row_block, weight_block, preferred_element_type=jnp.float32)
    hidden = jax.nn.gelu(pre_act, approximate=False).astype(jnp.bfloat16)
    return pool_rows(clip_onehot(clip_list, clip_count), hidden)


def local(frames_in, clip_ids, norm_gain, expand_weight, reduce_weight, conn_gain, conn_weight):
    devices_row = lax.axis_size("row")
    tok_local = frames_in.shape[0]
    clip_count = devices_row * (tok_local // FRAMES)
    width_local = expand_weight.shape[1]
    normed = layer_norm(frames_in.astype(jnp.float32), norm_gain).astype(jnp.bfloat16)
    residual = pool_rows(clip_onehot(clip_ids, clip_count), frames_in) / FRAMES
    spread = 4
    quarter = tok_local // spread
    repeats = devices_row // spread
    position = lax.axis_index("row")
    row_parts = normed.reshape(spread, quarter, -1)
    id_parts = clip_ids.reshape(spread, quarter)
    bit_list = [0, 1]
    part_index = position % spread
    send_rows = jnp.tile(row_parts, (repeats, 1, 1)).reshape(devices_row * quarter, -1)
    send_ids = jnp.tile(id_parts, (repeats, 1)).reshape(devices_row * quarter)
    my_rows, my_ids = (
        lax.all_to_all(send_rows, "row", split_axis=0, concat_axis=0, tiled=True),
        lax.all_to_all(send_ids, "row", split_axis=0, concat_axis=0, tiled=True),
    )
    group_cols = expand_weight
    for bit in bit_list:
        received = swapped(group_cols, "row", bit)
        upper = position // 2**bit % 2 == 1
        group_cols = jnp.concatenate(
            [jnp.where(upper, received, group_cols), jnp.where(upper, group_cols, received)], axis=1
        )
    partial_pool = hidden_pool(my_rows, my_ids, group_cols, clip_count)
    for bit in bit_list:
        partial_pool = partial_pool + swapped(partial_pool, "row", bit)
    summed = lax.dynamic_slice_in_dim(partial_pool, part_index * width_local, width_local, 1)
    pooled_hidden = (summed / FRAMES).astype(jnp.bfloat16)
    partial_value = residual + jnp.dot(
        pooled_hidden, reduce_weight, preferred_element_type=jnp.float32
    )
    owned_rows = lax.psum_scatter(partial_value, "row", scatter_dimension=0, tiled=True)
    connected = layer_norm(owned_rows, conn_gain).astype(jnp.bfloat16)
    every_clip = lax.all_gather(connected, "row", axis=0, tiled=True)
    projected = jnp.dot(every_clip, conn_weight, preferred_element_type=jnp.float32).astype(
        jnp.bfloat16
    )
    return lax.all_to_all(projected, "row", split_axis=0, concat_axis=1, tiled=True)


def solution(mesh):
    in_specs = (
        P(("groups", "row"), None),
        P(("groups", "row")),
        P(),
        P(None, "row"),
        P("row", None),
        P(),
        P(None, "row"),
    )
    out_specs = P(("groups", "row"), None)
    return jax.shard_map(local, mesh=mesh, in_specs=in_specs, out_specs=out_specs, check_vma=False)
```

profile of v0, /device:TPU:0, one launch (start us, length us, event | category | flops | bytes accessed | tf_op | source)
XLA Modules:
  0.0 1169.4 jit_solution(12103244747416812138)
XLA Ops:
  6.5 0.5 collective-permute-start
  7.0 28.1 %collective-permute-done = bf16[6144,1536]{1,0:T(8,128)(2,1)} collective-permute-done((bf16[6144,1536]{1,0:T(8,128)(2,1)}, bf16[6144,1536]{1,0:T(8,128)(2,1)}, u32[]{:S(2)}, u32[]{:S(2)}) %collective-permute-start) | collective-permute-done | bytes 18874400 | tf_op jit(solution)/shard_map/ppermute | solution.py:13
  35.2 26.2 %broadcast_select_fusion.3 = (bf16[6144,1536]{1,0:T(8,128)(2,1)}, bf16[6144,1536]{1,0:T(8,128)(2,1)}) fusion(bf16[6144,1536]{1,0:T(8,128)(2,1)} %collective-permute-done, bf16[6144,1536]{1,0:T(8,128)(2,1)} %param.10, pred[]{:T(512)S(6)} %eq.46), kind=kLoop, calls=%fused_computation.8 | loop fusion | flops 18874368 | bytes 75497472 | tf_op jit(solution)/shard_map/jit(_where)/select_n | solution.py:67
  61.4 25.5 %pad_maximum_fusion = bf16[6144,3072]{1,0:T(8,128)(2,1)} fusion(bf16[6144,1536]{1,0:T(8,128)(2,1)} %get-tuple-element.8, bf16[6144,1536]{1,0:T(8,128)(2,1)} %get-tuple-element.7), kind=kLoop, calls=%fused_computation.4 | loop fusion | flops 75497472 | bytes 75497472 | tf_op jit(solution)/shard_map/concatenate | solution.py:66
  86.9 2.9 collective-permute-start.1
  89.9 0.6 tile.19.clone
  90.5 5.0 all-to-all-start
  96.2 804.0 %all-to-all-done = s32[16,4,1]{1,2,0:T(1,128)S(1)} async-done(((s32[16,4,1]{1,2,0:T(1,128)}), s32[16,4,1]{1,2,0:T(1,128)S(1)}, u32[]{:S(2)}, u32[]{:S(2)}) %all-to-all-start) | async-done | bytes 288 | tf_op jit(solution)/shard_map/all_to_all | solution.py:60
  900.2 1.2 tile.22
  901.4 6.2 all-to-all-start.1
  907.7 0.5 broadcast.58
  908.2 0.7 reduce.5
  908.9 17.3 %all-to-all-done.1 = bf16[16,4,6144]{2,1,0:T(4,128)(2,1)S(1)} async-done(((bf16[16,4,6144]{2,1,0:T(4,128)(2,1)}), bf16[16,4,6144]{2,1,0:T(4,128)(2,1)S(1)}, u32[]{:S(2)}, u32[]{:S(2)}) %all-to-all-start.1) | async-done | bytes 786464 | tf_op jit(solution)/shard_map/all_to_all | solution.py:59
  926.4 49.4 %broadcast_select_fusion.1 = (bf16[6144,3072]{1,0:T(8,128)(2,1)}, bf16[6144,3072]{1,0:T(8,128)(2,1)}) fusion(bf16[6144,3072]{1,0:T(8,128)(2,1)} %collective-permute-done.1, pred[]{:T(512)S(6)} %eq.45, bf16[6144,1536]{1,0:T(8,128)(2,1)} %get-tuple-element.8, bf16[6144,1536]{1,0:T(8,128)(2,1)} %get-tuple-element.7), kind=kLoop, calls=%fused_computation.6 | loop fusion | flops 113246208 | bytes 150994944 | tf_op jit(solution)/shard_map/jit(_where)/select_n | solution.py:67
  975.8 28.5 %fusion.6.clone.5 = bf16[64,6144]{1,0:T(8,128)(2,1)S(1)} fusion(bf16[64,6144]{1,0:T(8,128)(2,1)S(1)} %all_to_all.24, bf16[6144,3072]{1,0:T(8,128)(2,1)} %get-tuple-element.6, bf16[6144,3072]{1,0:T(8,128)(2,1)} %get-tuple-element.5), kind=kOutput, calls=%fused_computation.14.clone.clone.clone.2 | convolution fusion | flops 5008392192 | bytes 77070336 | tf_op jit(solution)/shard_map/dot_general | solution.py:36
  1004.3 0.3 fusion.18
  1004.7 0.4 collective-permute-start.2
  1005.1 1.4 collective-permute-done.2
  1006.5 1.7 collective-permute-start.3
  1008.5 9.4 collective-permute-done.3
  1017.9 9.7 convolution_add_fusion
  1027.7 0.6 dynamic-slice
  1028.2 91.7 %all-reduce.3.cloned.1.call-done = f32[16,6144]{1,0:T(8,128)} async-done(((f32[16,6144]{1,0:T(8,128)}), f32[16,6144]{1,0:T(8,128)}) %all-reduce.3.cloned.1.call-update) | async-done | bytes 393232
  1119.9 2.3 dynamic-slice_reduce_fusion
  1122.9 2.3 multiply_reduce_fusion
  1125.8 1.6 convert_bitcast_fusion
  1127.5 20.4 %all-gather = bf16[16,1,6144]{2,1,0:T(2,128)(2,1)S(1)} all-gather(bf16[1,1,6144]{2,1,0:T(2,128)(2,1)S(1)} %convert_bitcast_fusion), channel_id=1, replica_groups=mesh['groups'=2,'row'=16] {'row'}, dimensions={0}, use_global_device_ids=true | all-gather | bytes 208896 | tf_op jit(solution)/shard_map/all_gather | solution.py:79
  1147.9 3.7 fusion.16
  1151.6 0.5 broadcast.63
  1152.1 0.7 reduce.6
  1152.8 9.1 all_to_all.31
  1161.9 0.6 reshape.69
  (25 shorter events, 1.5 us)
Async XLA Ops:
  6.5 28.6 %collective-permute-start = (bf16[6144,1536]{1,0:T(8,128)(2,1)}, bf16[6144,1536]{1,0:T(8,128)(2,1)}, u32[]{:S(2)}, u32[]{:S(2)}) collective-permute-start(bf16[6144,1536]{1,0:T(8,128)(2,1)} %param.10), channel_id=1, source_target_pairs={{0,1},{1,0},{2,3},{3,2},{4,5},{5,4},{6,7},{7,6},{8,9},{9,8},{10,11... | collective-permute-start | bytes 56623112 | tf_op jit(solution)/shard_map/ppermute | solution.py:13
  61.4 28.5 %copy-start.3 = (s32[16]{0:T(128)S(1)}, s32[16]{0:T(128)}, u32[]{:S(2)}) copy-start(s32[16]{0:T(128)} %param.8) | copy-start | bytes 196
  61.4 34.1 %copy-start = (bf16[16,6144]{1,0:T(8,128)(2,1)S(1)}, bf16[16,6144]{1,0:T(8,128)(2,1)}, u32[]{:S(2)}) copy-start(bf16[16,6144]{1,0:T(8,128)(2,1)} %param.7) | copy-start | bytes 589828
  61.4 34.6 %copy-start.1 = (f32[6144]{0:T(1024)S(1)}, f32[6144]{0:T(1024)}, u32[]{:S(2)}) copy-start(f32[6144]{0:T(1024)} %param.9) | copy-start | bytes 73732
  86.9 839.5 %collective-permute-start.1 = (bf16[6144,3072]{1,0:T(8,128)(2,1)}, bf16[6144,3072]{1,0:T(8,128)(2,1)}, u32[]{:S(2)}, u32[]{:S(2)}) collective-permute-start(bf16[6144,3072]{1,0:T(8,128)(2,1)} %pad_maximum_fusion), channel_id=1, source_target_pairs={{0,2},{1,3},{2,0},{3,1},{4,6},{5,7},{6,4},{7,5},{8,10},{9,11},{10,... | collective-permute-start | bytes 113246216 | tf_op jit(solution)/shard_map/ppermute | solution.py:13
  90.5 809.6 %all-to-all-start = ((s32[16,4,1]{1,2,0:T(1,128)}), s32[16,4,1]{1,2,0:T(1,128)S(1)}, u32[]{:S(2)}, u32[]{:S(2)}) async-start(s32[16,4,1]{1,2,0:T(1,128)} %bitcast), calls=%async_computation | async-start | bytes 16384 | tf_op jit(solution)/shard_map/all_to_all | solution.py:60
  901.4 24.8 %all-to-all-start.1 = ((bf16[16,4,6144]{2,1,0:T(4,128)(2,1)}), bf16[16,4,6144]{2,1,0:T(4,128)(2,1)S(1)}, u32[]{:S(2)}, u32[]{:S(2)}) async-start(bf16[16,4,6144]{2,1,0:T(4,128)(2,1)} %bitcast.1), calls=%async_computation.1 | async-start | bytes 1572864 | tf_op jit(solution)/shard_map/all_to_all | solution.py:59
  907.6 212.4 %all-reduce.3.cloned.1.call-start = ((), (), s32[]{:S(2)}) async-start(), calls=%async_computation.3 | async-start | bytes 786432
  1004.7 1.8 collective-permute-start.2
  1006.5 11.4 collective-permute-start.3
  1008.5 19.2 %copy-start.4 = (u32[32]{0:T(128)S(1)}, u32[32]{0:T(128)}, u32[]{:S(2)}) copy-start(u32[32]{0:T(128)} %constant.139) | copy-start | bytes 388
  1008.5 117.3 %copy-start.2 = (f32[6144]{0:T(1024)S(1)}, f32[6144]{0:T(1024)}, u32[]{:S(2)}) copy-start(f32[6144]{0:T(1024)} %param.12) | copy-start | bytes 73732
Sparse Core Ops, SparseCore 0:
  1027.8 92.1 all-reduce.2
where the time goes:
time: 1170 us
  waiting for transfers between devices  952 us (81%)
  other arithmetic  109 us (9%)
  matrix products  42.5 us (4%)
  blocking collectives  29.5 us (3%)
  starting transfers between devices  16.7 us (1%)
  between operations  14.9 us (1%)
    all_to_all x1, waiting for transfers between devices, local(): lax.all_to_all(send_ids, 'row', split_axis=0, concat_axis=0, tiled=True)  804 us
    unnamed x2, waiting for transfers between devices  91.7 us
    select_n x2, other arithmetic, local(): jnp.where(upper, received, group_cols)  75.6 us
    ppermute x4, waiting for transfers between devices, swapped(): lax.ppermute(shard, axis, [(i, i ^ 1 << distance) for i in range(lax.axis...  38.9 us
    dot_general x1, matrix products, hidden_pool(): jnp.dot(row_block, weight_block, preferred_element_type=jnp.float32)  28.5 us
    concatenate x1, other arithmetic, local(): jnp.concatenate([jnp.where(upper, received, group_cols), jnp.where(upper,...  25.5 us
  transfers between devices with their start and end apart: 7, of which 6 were waited for; matrix products, arithmetic and copies ran while one was open for 0% of the time, Pallas kernels for 0%

commit v1 on v0

--- a/solution.py
+++ b/solution.py
@@ -7,10 +7,6 @@
 
 
 epsilon = 1e-06
-
-
-def swapped(shard, axis, distance):
-    return lax.ppermute(shard, axis, [(i, i ^ 1 << distance) for i in range(lax.axis_size(axis))])
 
 
 def layer_norm(values, gain_row):
@@ -42,34 +38,11 @@
     devices_row = lax.axis_size("row")
     tok_local = frames_in.shape[0]
     clip_count = devices_row * (tok_local // FRAMES)
-    width_local = expand_weight.shape[1]
     normed = layer_norm(frames_in.astype(jnp.float32), norm_gain).astype(jnp.bfloat16)
     residual = pool_rows(clip_onehot(clip_ids, clip_count), frames_in) / FRAMES
-    spread = 4
-    quarter = tok_local // spread
-    repeats = devices_row // spread
-    position = lax.axis_index("row")
-    row_parts = normed.reshape(spread, quarter, -1)
-    id_parts = clip_ids.reshape(spread, quarter)
-    bit_list = [0, 1]
-    part_index = position % spread
-    send_rows = jnp.tile(row_parts, (repeats, 1, 1)).reshape(devices_row * quarter, -1)
-    send_ids = jnp.tile(id_parts, (repeats, 1)).reshape(devices_row * quarter)
-    my_rows, my_ids = (
-        lax.all_to_all(send_rows, "row", split_axis=0, concat_axis=0, tiled=True),
-        lax.all_to_all(send_ids, "row", split_axis=0, concat_axis=0, tiled=True),
-    )
-    group_cols = expand_weight
-    for bit in bit_list:
-        received = swapped(group_cols, "row", bit)
-        upper = position // 2**bit % 2 == 1
-        group_cols = jnp.concatenate(
-            [jnp.where(upper, received, group_cols), jnp.where(upper, group_cols, received)], axis=1
-        )
-    partial_pool = hidden_pool(my_rows, my_ids, group_cols, clip_count)
-    for bit in bit_list:
-        partial_pool = partial_pool + swapped(partial_pool, "row", bit)
-    summed = lax.dynamic_slice_in_dim(partial_pool, part_index * width_local, width_local, 1)
+    every_row = lax.all_gather(normed, "row", axis=0, tiled=True)
+    every_id = lax.all_gather(clip_ids, "row", axis=0, tiled=True)
+    summed = hidden_pool(every_row, every_id, expand_weight, clip_count)
     pooled_hidden = (summed / FRAMES).astype(jnp.bfloat16)
     partial_value = residual + jnp.dot(
         pooled_hidden, reduce_weight, preferred_element_type=jnp.float32

time: 1170 us -> 219 us (0.19)
  waiting for transfers between devices: 952 us -> 120 us
  other arithmetic: 109 us -> 10.9 us
  matrix products: 42.5 us -> 25.6 us
  starting transfers between devices: 16.7 us -> 0.04 us
  blocking collectives: 29.5 us -> 43.2 us
    all_to_all x2 -> x0, waiting for transfers between devices: 821 us -> none  [the longest x1 804 us: local(): lax.all_to_all(send_ids, 'row', split_axis=0, concat_axis=0, tiled=True)]
    select_n x2 -> x0, other arithmetic: 75.6 us -> none  [local(): jnp.where(upper, received, group_cols)]
    ppermute x4 -> x0, waiting for transfers between devices: 38.9 us -> none  [swapped(): lax.ppermute(shard, axis, [(i, i ^ 1 << distance) for i in range(lax.axis...]
    all_gather x0 -> x1, waiting for transfers between devices: none -> 30.4 us  [local(): every_row = lax.all_gather(normed, 'row', axis=0, tiled=True)]
    concatenate x1 -> x0, other arithmetic: 25.5 us -> none  [local(): jnp.concatenate([jnp.where(upper, received, group_cols), jnp.where(upper,...]
    dot_general x1, matrix products: 28.5 us -> 9.97 us  [hidden_pool(): jnp.dot(row_block, weight_block, preferred_element_type=jnp.float32)]
    unnamed x0 -> x1, blocking collectives: none -> 13.7 us
    unnamed x2 -> x3, waiting for transfers between devices: 91.7 us -> 89.9 us
  transfers between devices with their start and end apart: 7 -> 2, of which waited for: 6 -> 2; matrix products, arithmetic and copies ran while one was open for 0% -> 2% of each run, Pallas kernels for 0% -> 0%
where the time goes in v1:
time: 219 us
  waiting for transfers between devices  120 us (55%)
  blocking collectives  43.2 us (20%)
  matrix products  25.6 us (12%)
  between operations  15.4 us (7%)
  other arithmetic  10.9 us (5%)
  local copies, waits for them, and re-layouts  3.43 us (2%)
    unnamed x3, waiting for transfers between devices  89.9 us
    all_gather x1, waiting for transfers between devices, local(): every_row = lax.all_gather(normed, 'row', axis=0, tiled=True)  30.4 us
    all_gather x1, blocking collectives, local(): every_clip = lax.all_gather(connected, 'row', axis=0, tiled=True)  20.4 us
    unnamed x1, blocking collectives  13.7 us
    dot_general x1, matrix products, local(): jnp.dot(pooled_hidden, reduce_weight, preferred_element_type=jnp.float32)  10.6 us
    dot_general x1, matrix products, hidden_pool(): jnp.dot(row_block, weight_block, preferred_element_type=jnp.float32)  9.97 us
    all_to_all x1, blocking collectives, local(): lax.all_to_all(projected, 'row', split_axis=0, concat_axis=1, tiled=True)  9.07 us
  transfers between devices with their start and end apart: 2, of which 2 were waited for; matrix products, arithmetic and copies ran while one was open for 2% of the time, Pallas kernels for 0%

profile of v1, /device:TPU:0, one launch (start us, length us, event | category | flops | bytes accessed | tf_op | source)
XLA Modules:
  0.0 218.9 jit_solution(4393564919716177675)
XLA Ops:
  6.5 0.0 all-gather.3.cloned.1.call-start
  6.5 1.1 convert_reduce_fusion
  7.6 1.2 fusion.74
  8.8 1.7 fusion.76
  10.5 0.0 all-gather.3.cloned.1.call-update
  10.6 0.0 all-reduce.4.cloned.1.call-start
  10.6 1.4 fusion.144
  12.7 0.9 dynamic-update-slice
  13.5 13.7 %all-reduce = s32[256]{0:T(256)S(1)} all-reduce(s32[256]{0:T(256)S(1)} %dynamic-update-slice), channel_id=1, replica_groups=mesh['groups'=2,'row'=16] {'row'}, use_global_device_ids=true, to_apply=%add | all-reduce | flops 256 | bytes 2048
  27.3 1.3 convolution_multiply_fusion
  28.5 30.4 %all-gather.3.cloned.1.call-done = bf16[256,6144]{1,0:T(8,128)(2,1)} async-done(((bf16[16,6144]{1,0:T(8,128)(2,1)}), bf16[256,6144]{1,0:T(8,128)(2,1)}) %all-gather.3.cloned.1.call-update) | async-done | bytes 3145744 | tf_op jit(solution)/shard_map/all_gather | solution.py:43
  58.9 10.0 %fusion.145 = f32[256,1536]{1,0:T(8,128)S(1)} fusion(bf16[256,6144]{1,0:T(8,128)(2,1)} %all-gather.3.cloned.1.call-done, bf16[6144,1536]{1,0:T(8,128)(2,1)} %param.10), kind=kOutput, calls=%fused_computation.105 | convolution fusion | flops 4831838208 | bytes 23592960 | tf_op jit(solution)/shard_map/dot_general | solution.py:32
  68.9 0.0 copy-start
  68.9 10.6 %convolution_add_fusion = f32[16,6144]{1,0:T(8,128)} fusion(f32[16,6144]{1,0:T(8,128)S(1)} %convolution_multiply_fusion, bf16[1536,6144]{1,0:T(8,128)(2,1)} %param.11, f32[256,1536]{1,0:T(8,128)S(1)} %fusion.145, s32[256]{0:T(256)S(1)} %all-reduce), kind=kOutput, calls=%fused_computation | convolution fusion | flops 340283392 | bytes 21234688 | tf_op jit(solution)/shard_map/dot_general | solution.py:47
  79.5 0.0 all-reduce.4.cloned.1.call-update
  79.6 89.9 %all-reduce.4.cloned.1.call-done = f32[16,6144]{1,0:T(8,128)} async-done(((f32[16,6144]{1,0:T(8,128)}), f32[16,6144]{1,0:T(8,128)}) %all-reduce.4.cloned.1.call-update) | async-done | bytes 393232
  169.5 2.3 %dynamic-slice_reduce_fusion = f32[]{:T(128)} fusion(f32[16,6144]{1,0:T(8,128)} %all-reduce.4.cloned.1.call-done, u32[]{:T(128)} %bitcast.5), kind=kLoop, calls=%fused_computation.70 | loop fusion | flops 6143 | bytes 24584 | tf_op jit(solution)/shard_map/reduce_sum | solution.py:13
  172.4 2.3 %multiply_reduce_fusion = f32[]{:T(128)} fusion(f32[]{:T(128)S(6)} %div.30, f32[16,6144]{1,0:T(8,128)} %all-reduce.4.cloned.1.call-done, u32[]{:T(128)} %bitcast.5), kind=kLoop, calls=%fused_computation.67 | loop fusion | flops 18431 | bytes 24588 | tf_op jit(solution)/shard_map/reduce_sum | solution.py:15
  175.4 0.0 copy-done
  175.4 1.6 convert_bitcast_fusion
  177.0 20.4 %all-gather = bf16[16,1,6144]{2,1,0:T(2,128)(2,1)S(1)} all-gather(bf16[1,1,6144]{2,1,0:T(2,128)(2,1)S(1)} %convert_bitcast_fusion), channel_id=1, replica_groups=mesh['groups'=2,'row'=16] {'row'}, dimensions={0}, use_global_device_ids=true | all-gather | bytes 208896 | tf_op jit(solution)/shard_map/all_gather | solution.py:52
  197.4 3.7 %fusion.11 = bf16[16,1,512]{2,0,1:T(8,128)(2,1)S(1)} fusion(bf16[6144,512]{1,0:T(8,128)(2,1)} %param.13, bf16[16,1,6144]{2,1,0:T(2,128)(2,1)S(1)} %all-gather), kind=kOutput, calls=%fused_computation.24 | convolution fusion | flops 100671488 | bytes 6504448 | tf_op jit(solution)/shard_map/dot_general | solution.py:53
  201.1 0.5 broadcast.47
  201.7 0.7 reduce.2
  202.3 9.1 %all_to_all.16 = bf16[16,2,256]{2,1,0:T(2,128)(2,1)S(1)} all-to-all(bf16[16,2,256]{2,1,0:T(2,128)(2,1)S(1)} %reshape.46), channel_id=1, replica_groups=mesh['groups'=2,'row'=16] {'row'}, dimensions={0} | all-to-all | bytes 32768 | tf_op jit(solution)/shard_map/all_to_all | solution.py:56
  211.4 0.6 reshape.47
  (4 shorter events, 0.0 us)
Async XLA Ops:
  6.5 52.4 %all-gather.3.cloned.1.call-start = ((), (), s32[]{:S(2)}) async-start(), calls=%async_computation.1 | async-start | bytes 3342336 | tf_op jit(solution)/shard_map/all_gather | solution.py:43
  10.6 158.9 %all-reduce.4.cloned.1.call-start = ((), (), s32[]{:S(2)}) async-start(), calls=%async_computation.2 | async-start | bytes 786432
  68.9 106.4 %copy-start = (f32[6144]{0:T(1024)S(1)}, f32[6144]{0:T(1024)}, u32[]{:S(2)}) copy-start(f32[6144]{0:T(1024)} %param.12) | copy-start | bytes 73732
Sparse Core Ops, SparseCore 0:
  10.7 48.1 all-gather.2
  79.7 89.7 all-reduce.3

commit v2 on v1

--- a/solution.py
+++ b/solution.py
@@ -1,11 +1,15 @@
+import functools
+
 import jax
 import jax.numpy as jnp
 from jax import lax
+from jax.experimental import pallas as pl
+from jax.experimental.pallas import tpu as pltpu
 from jax.sharding import PartitionSpec as P
 
 FRAMES = 16
-
-
+LANES = 128
+MESH = pl.DeviceIdType.MESH
 epsilon = 1e-06
 
 
@@ -34,7 +38,7 @@
     return pool_rows(clip_onehot(clip_list, clip_count), hidden)
 
 
-def local(frames_in, clip_ids, norm_gain, expand_weight, reduce_weight, conn_gain, conn_weight):
+def plain(frames_in, clip_ids, norm_gain, expand_weight, reduce_weight, conn_gain, conn_weight):
     devices_row = lax.axis_size("row")
     tok_local = frames_in.shape[0]
     clip_count = devices_row * (tok_local // FRAMES)
@@ -56,6 +60,261 @@
     return lax.all_to_all(projected, "row", split_axis=0, concat_axis=1, tiled=True)
 
 
+def copy_block(buf, block, send, slot, recv, to):
+    return pltpu.make_async_remote_copy(
+        src_ref=buf.at[block],
+        dst_ref=buf.at[block],
+        send_sem=send.at[slot],
+        recv_sem=recv.at[block],
+        device_id={"row": to},
+        device_id_type=MESH,
+    )
+
+
+def spread_blocks(buf, send, recv, n, me):
+    core, chip = me % 2, me // 2
+    x, z, depth = chip % 2, chip // 2, n // 4
+    partner = chip * 2 + (1 - core)
+    beside = (z * 2 + 1 - x) * 2 + core
+    started = []
+
+    def go(block, to):
+        copy = copy_block(buf, block, send, len(started), recv, to)
+        copy.start()
+        started.append(copy)
+
+    def arrive(block):
+        copy_block(buf, block, send, 0, recv, partner).wait_recv()
+
+    go(me, beside)
+    for step in range(1, depth):
+        go(me, (((z + step) % depth) * 2 + x) * 2 + core)
+    go(me, partner)
+    arrive(beside)
+    go(beside, partner)
+    for step in range(1, depth):
+        block = (((z + depth - step) % depth) * 2 + x) * 2 + core
+        arrive(block)
+        go(block, beside)
+        go(block, partner)
+    for step in range(1, depth):
+        block = (((z + depth - step) % depth) * 2 + 1 - x) * 2 + core
+        arrive(block)
+        go(block, partner)
+    for other in range(n // 2):
+        arrive(other * 2 + 1 - core)
+    return started
+
+
+def kernel(
+    n, frames_ref, idcol_ref, idrow_ref, ngain_ref, w1_hbm, w2_hbm, cgain_ref, w3_hbm, out_ref,
+    rows, w1, w2, w3, onehot_t, ph, part, landed, red, conn, proj, arrived,
+    w_sem, g_send, g_recv, r_send, r_recv, a_send, a_recv, o_send, o_recv,
+):
+    me = lax.axis_index("row")
+    tok, dim = frames_ref.shape
+    clips = ph.shape[0]
+    width = w1.shape[1]
+    bw = part.shape[2]
+    ew = w3.shape[1]
+    barrier = pltpu.get_barrier_semaphore()
+    for step in range(1, n):
+        pl.semaphore_signal(
+            barrier, inc=1, device_id={"row": (me + step) % n}, device_id_type=MESH
+        )
+    loads = []
+    for index, (src, dst) in enumerate(((w1_hbm, w1), (w2_hbm, w2), (w3_hbm, w3))):
+        tall = src.shape[0] // 4
+        group = []
+        for piece in range(4):
+            span = pl.ds(piece * tall, tall)
+            load = pltpu.make_async_copy(src.at[span], dst.at[span], w_sem.at[index, piece])
+            load.start()
+            group.append(load)
+        loads.append(group)
+
+    normed = layer_norm(frames_ref[...].astype(jnp.float32), ngain_ref[...])
+    rows[me, :, 0:dim] = normed.astype(jnp.bfloat16)
+    rows[me, :, dim : dim + LANES] = idcol_ref[...].astype(jnp.float32).astype(jnp.bfloat16)
+    pl.semaphore_wait(barrier, n - 1)
+    sent = spread_blocks(rows, g_send, g_recv, n, me)
+
+    every_id = rows[:, :, dim : dim + LANES].reshape(n * tok, LANES).astype(jnp.float32)
+    lane = lax.broadcasted_iota(jnp.int32, (n * tok, LANES), 1).astype(jnp.float32)
+    onehot = jnp.where(every_id == lane, 1.0, 0.0)
+    onehot_t[...] = jnp.transpose(onehot)[0:clips].astype(jnp.bfloat16)
+    for load in loads[0]:
+        load.wait()
+    cw = 256
+
+    @pl.loop(0, width // cw)
+    def _(step):
+        cols = pl.ds(pl.multiple_of(step * cw, cw), cw)
+        pre_act = jnp.dot(
+            rows[:, :, 0:dim].reshape(n * tok, dim), w1[:, cols], preferred_element_type=jnp.float32
+        )
+        hidden = 0.5 * pre_act * (1.0 + lax.erf(pre_act * 0.7071067811865476))
+        summed = jnp.dot(
+            onehot_t[...], hidden.astype(jnp.bfloat16), preferred_element_type=jnp.float32
+        )
+        ph[:, cols] = (summed / FRAMES).astype(jnp.bfloat16)
+
+    for copy in sent:
+        copy.wait_send()
+    for load in loads[1]:
+        load.wait()
+    own_hot = jnp.where(
+        lax.broadcasted_iota(jnp.int32, (clips, tok), 0) == idrow_ref[...], 1.0, 0.0
+    ).astype(jnp.bfloat16)
+
+    def term(owner):
+        cols = pl.ds(pl.multiple_of(owner * bw, LANES), bw)
+        residual = jnp.dot(own_hot, frames_ref[:, cols], preferred_element_type=jnp.float32)
+        return residual / FRAMES + jnp.dot(
+            ph[...], w2[:, cols], preferred_element_type=jnp.float32
+        )
+
+    def give(step):
+        owner = (me + 1 + step) % n
+        return pltpu.make_async_remote_copy(
+            src_ref=part.at[owner],
+            dst_ref=landed.at[me],
+            send_sem=r_send.at[step],
+            recv_sem=r_recv.at[me],
+            device_id={"row": owner},
+            device_id_type=MESH,
+        )
+
+    @pl.loop(0, n - 1)
+    def _(step):
+        owner = (me + 1 + step) % n
+        part[owner] = term(owner)
+
+        @pl.when(step > 0)
+        def _():
+            give(step - 1).start()
+
+    total = term(me)
+    give(n - 2).start()
+    for step in range(1, n):
+        source = (me + n - step) % n
+        pltpu.make_async_remote_copy(
+            src_ref=part.at[source],
+            dst_ref=landed.at[source],
+            send_sem=r_send.at[0],
+            recv_sem=r_recv.at[source],
+            device_id={"row": source},
+            device_id_type=MESH,
+        ).wait_recv()
+        total = total + landed[source]
+    red[me] = total
+    for step in range(n - 1):
+        give(step).wait_send()
+    sent = spread_blocks(red, a_send, a_recv, n, me)
+
+    pooled = red[...]
+    average = jnp.sum(jnp.sum(pooled, axis=0), axis=-1, keepdims=True) / dim
+    centered = pooled - average[None]
+    variance = jnp.sum(jnp.sum(centered * centered, axis=0), axis=-1, keepdims=True) / dim
+    scale = lax.rsqrt(variance + epsilon)
+    for block in range(n):
+        cols = slice(block * bw, (block + 1) * bw)
+        conn[:, cols] = ((red[block] - average) * scale * cgain_ref[:, cols]).astype(jnp.bfloat16)
+    for load in loads[2]:
+        load.wait()
+    projected = jnp.dot(conn[...], w3[...], preferred_element_type=jnp.float32)
+    for clip in range(clips):
+        proj[clip] = projected[clip : clip + 1]
+    arrived[pl.ds(me, 1)] = proj[pl.ds(me, 1)]
+    for copy in sent:
+        copy.wait_send()
+    outs = []
+    for step in range(1, n):
+        owner = (me + step) % n
+        copy = pltpu.make_async_remote_copy(
+            src_ref=proj.at[owner],
+            dst_ref=arrived.at[me],
+            send_sem=o_send.at[step],
+            recv_sem=o_recv.at[me],
+            device_id={"row": owner},
+            device_id_type=MESH,
+        )
+        copy.start()
+        outs.append(copy)
+    for step in range(1, n):
+        source = (me + n - step) % n
+        pltpu.make_async_remote_copy(
+            src_ref=proj.at[source],
+            dst_ref=arrived.at[source],
+            send_sem=o_send.at[0],
+            recv_sem=o_recv.at[source],
+            device_id={"row": source},
+            device_id_type=MESH,
+        ).wait_recv()
+    for block in range(n):
+        out_ref[:, block * ew : (block + 1) * ew] = arrived[block].astype(jnp.bfloat16)
+    for copy in outs:
+        copy.wait_send()
+
+
+def fused(frames_in, clip_ids, norm_gain, expand_weight, reduce_weight, conn_gain, conn_weight):
+    n = lax.axis_size("row")
+    tok, dim = frames_in.shape
+    width, ew = expand_weight.shape[1], conn_weight.shape[1]
+    bw = dim // n
+    vmem, hbm = pl.BlockSpec(memory_space=pltpu.VMEM), pl.BlockSpec(memory_space=pl.ANY)
+    dma = pltpu.SemaphoreType.DMA
+    f32, bf16 = jnp.float32, jnp.bfloat16
+    return pl.pallas_call(
+        functools.partial(kernel, n),
+        name="vision_block",
+        out_shape=jax.ShapeDtypeStruct((1, n * ew), bf16),
+        in_specs=[vmem, vmem, vmem, vmem, hbm, hbm, vmem, hbm],
+        out_specs=vmem,
+        scratch_shapes=[
+            pltpu.VMEM((n, tok, dim + LANES), bf16),
+            pltpu.VMEM((dim, width), bf16),
+            pltpu.VMEM((width, dim), bf16),
+            pltpu.VMEM((dim, ew), bf16),
+            pltpu.VMEM((n, n * tok), bf16),
+            pltpu.VMEM((n, width), bf16),
+            pltpu.VMEM((n, n, bw), f32),
+            pltpu.VMEM((n, n, bw), f32),
+            pltpu.VMEM((n, n, bw), f32),
+            pltpu.VMEM((n, dim), bf16),
+            pltpu.VMEM((n, 1, ew), f32),
+            pltpu.VMEM((n, 1, ew), f32),
+            dma((3, 4)),
+            dma((n,)), dma((n,)), dma((n,)), dma((n,)),
+            dma((n,)), dma((n,)), dma((n,)), dma((n,)),
+        ],
+        compiler_params=pltpu.CompilerParams(
+            collective_id=0, has_side_effects=True, vmem_limit_bytes=60 * 1024 * 1024
+        ),
+    )(
+        frames_in,
+        jnp.broadcast_to(clip_ids[:, None], (tok, LANES)),
+        clip_ids[None, :],
+        norm_gain[None, :],
+        expand_weight,
+        reduce_weight,
+        conn_gain[None, :],
+        conn_weight,
+    )
+
+
+def local(frames_in, clip_ids, norm_gain, expand_weight, reduce_weight, conn_gain, conn_weight):
+    n = lax.axis_size("row")
+    tok, dim = frames_in.shape
+    width, ew = expand_weight.shape[1], conn_weight.shape[1]
+    fits = tok == FRAMES and n % 16 == 0 and n <= LANES and (n * tok) % LANES == 0
+    even = dim % (n * LANES) == 0 and width % 256 == 0 and ew % LANES == 0
+    form = fused if fits and even else plain
+    return form(
+        frames_in, clip_ids, norm_gain, expand_weight, reduce_weight, conn_gain, conn_weight
+    )
+
+
 def solution(mesh):
     in_specs = (
         P(("groups", "row"), None),

time: 219 us -> 69.6 us (0.32)
  waiting for transfers between devices: 120 us -> 0 us
  Pallas kernels: 0 us -> 66.7 us
  blocking collectives: 43.2 us -> 0 us
  matrix products: 25.6 us -> 0 us
  between operations: 15.4 us -> 0.01 us
  other arithmetic: 10.9 us -> 0 us
    unnamed x3 -> x0, waiting for transfers between devices: 89.9 us -> none
    pallas_call x0 -> x1, Pallas kernels: none -> 66.7 us  [fused(): pl.pallas_call(functools.partial(kernel, n), name='vision_block', out_sha...]
    all_gather x1 -> x0, waiting for transfers between devices: 30.4 us -> none  [local(): every_row = lax.all_gather(normed, 'row', axis=0, tiled=True)]
    dot_general x4 -> x0, matrix products: 25.6 us -> none  [the longest x1 10.6 us: local(): jnp.dot(pooled_hidden, reduce_weight, preferred_element_type=jnp.float32)]
    all_gather x1 -> x0, blocking collectives: 20.4 us -> none  [local(): every_clip = lax.all_gather(connected, 'row', axis=0, tiled=True)]
    unnamed x1 -> x0, blocking collectives: 13.7 us -> none
    all_to_all x1 -> x0, blocking collectives: 9.07 us -> none  [local(): lax.all_to_all(projected, 'row', split_axis=0, concat_axis=1, tiled=True)]
    reduce_sum x4 -> x0, other arithmetic: 6.84 us -> none  [the longest x2 3.46 us: layer_norm(): variance = jnp.mean(centered * centered, axis=-1, keepdims=True)]
  transfers between devices with their start and end apart: 2 -> 0, of which waited for: 2 -> 0; matrix products, arithmetic and copies ran while one was open for 2% -> 0% of each run, Pallas kernels for 0% -> 0%
where the time goes in v2:
time: 69.6 us; the launch traced here: 69.4 us
  Pallas kernels  66.7 us (96%)
  local copies, waits for them, and re-layouts  2.73 us (4%)
    pallas_call x1, Pallas kernels, fused(): pl.pallas_call(functools.partial(kernel, n), name='vision_block', out_sha...  66.7 us
    unnamed x1, local copies, waits for them, and re-layouts  1.41 us

profile of v2, /device:TPU:0, one launch (start us, length us, event | category | flops | bytes accessed | tf_op | source)
XLA Modules:
  0.0 69.4 jit_solution(11973039528849647906)
XLA Ops:
  0.0 1.3 %broadcast_in_dim.15.idcol_ref = s32[16,128]{1,0:T(8,128)} broadcast(s32[16]{0:T(128)} %param.8), dimensions={0} | broadcast | bytes 8256 | tf_op jit(solution)/shard_map/broadcast_in_dim | solution.py:296
  1.3 66.7 %vision_block.1 = bf16[1,8192]{1,0:T(2,128)(2,1)} custom-call(bf16[16,6144]{1,0:T(8,128)(2,1)} %frames_ref.1, s32[16,128]{1,0:T(8,128)} %broadcast_in_dim.15.idcol_ref, s32[1,16]{1,0:T(1,128)} %bitcast.5, f32[1,6144]{1,0:T(1,128)} %bitcast.3, bf16[6144,1536]{1,0:T(8,128)(2,1)} %w1_hbm.1, bf16[1536,6144]{1,0:T(8,128)(2,1)} %w2_hbm.1, f32[1,6144]{1,0:T(1,128)} %bitcast.4, ...), custom_call_target="tpu_custom_call" | custom-call | tf_op jit(solution)/shard_map/vision_block/pallas_call | solution.py:268
  68.0 1.4 %copy.9 = bf16[1,8192]{1,0:T(2,128)(2,1)} copy(bf16[1,8192]{1,0:T(2,128)(2,1)} %vision_block.1) | data formatting | bytes 32768

commit v3 on v2

--- a/solution.py
+++ b/solution.py
@@ -9,6 +9,7 @@
 
 FRAMES = 16
 LANES = 128
+PIECES = 2
 MESH = pl.DeviceIdType.MESH
 epsilon = 1e-06
 
@@ -107,8 +108,8 @@
 
 
 def kernel(
-    n, frames_ref, idcol_ref, idrow_ref, ngain_ref, w1_hbm, w2_hbm, cgain_ref, w3_hbm, out_ref,
-    rows, w1, w2, w3, onehot_t, ph, part, landed, red, conn, proj, arrived,
+    n, frames_ref, idrow_ref, ngain_ref, w1_hbm, w2_hbm, cgain_ref, w3_hbm, out_ref,
+    rows, acc, w1, w2, w3, onehot_t, ph, part, landed, red, conn, proj, arrived,
     w_sem, g_send, g_recv, r_send, r_recv, a_send, a_recv, o_send, o_recv,
 ):
     me = lax.axis_index("row")
@@ -124,9 +125,9 @@
         )
     loads = []
     for index, (src, dst) in enumerate(((w1_hbm, w1), (w2_hbm, w2), (w3_hbm, w3))):
-        tall = src.shape[0] // 4
+        tall = src.shape[0] // PIECES
         group = []
-        for piece in range(4):
+        for piece in range(PIECES):
             span = pl.ds(piece * tall, tall)
             load = pltpu.make_async_copy(src.at[span], dst.at[span], w_sem.at[index, piece])
             load.start()
@@ -135,32 +136,119 @@
 
     normed = layer_norm(frames_ref[...].astype(jnp.float32), ngain_ref[...])
     rows[me, :, 0:dim] = normed.astype(jnp.bfloat16)
-    rows[me, :, dim : dim + LANES] = idcol_ref[...].astype(jnp.float32).astype(jnp.bfloat16)
+    diagonal = lax.broadcasted_iota(jnp.int32, (tok, tok), 0) == lax.broadcasted_iota(
+        jnp.int32, (tok, tok), 1
+    )
+    own_ids = jnp.where(diagonal, idrow_ref[...].astype(jnp.float32), 0.0)
+    id_column = jnp.sum(own_ids, axis=1, keepdims=True)
+    rows[me, :, dim : dim + LANES] = jnp.broadcast_to(id_column, (tok, LANES)).astype(jnp.bfloat16)
     pl.semaphore_wait(barrier, n - 1)
-    sent = spread_blocks(rows, g_send, g_recv, n, me)
-
+
+    core, chip = me % 2, me // 2
+    x, z, depth = chip % 2, chip // 2, n // 4
+    partner = chip * 2 + (1 - core)
+    beside = (z * 2 + 1 - x) * 2 + core
+    deep = dim // PIECES
+    sent = []
+
+    def piece_copy(block, piece, slot, to):
+        end = dim + LANES if piece == PIECES - 1 else (piece + 1) * deep
+        spot = rows.at[block, :, piece * deep : end]
+        return pltpu.make_async_remote_copy(
+            src_ref=spot,
+            dst_ref=spot,
+            send_sem=g_send.at[slot],
+            recv_sem=g_recv.at[block, piece],
+            device_id={"row": to},
+            device_id_type=MESH,
+        )
+
+    def go(block, piece, to, when=True):
+        copy = piece_copy(block, piece, len(sent), to)
+        sent.append((copy, when))
+        if when is True:
+            copy.start()
+        else:
+            pl.when(when)(copy.start)
+
+    def arrive(block, piece):
+        piece_copy(block, piece, 0, partner).wait_recv()
+
+    hops = [(step, way) for step in range(1, depth) for way in (1, -1)]
+
+    def inside(level):
+        return jnp.logical_and(level >= 0, level < depth)
+
+    def rail(level, side):
+        return (level * 2 + side) * 2 + core
+
+    def finish(piece):
+        for step, way in hops:
+            origin = z - way * step
+            block = rail(origin, 1 - x)
+            pl.when(inside(origin))(functools.partial(arrive, block, piece))
+            go(block, piece, partner, inside(origin))
+        for other in range(n // 2):
+            arrive(other * 2 + 1 - core, piece)
+        loads[0][piece].wait()
+
+    cw = 256
+
+    def product(piece, cols):
+        span = slice(piece * deep, (piece + 1) * deep)
+        return jnp.dot(
+            rows[:, :, span].reshape(n * tok, deep), w1[span, cols], preferred_element_type=jnp.float32
+        )
+
+    for piece in range(PIECES):
+        go(me, piece, beside)
+        for way in (1, -1):
+            go(me, piece, rail(z + way, x), inside(z + way))
+        go(me, piece, partner)
+    for piece in range(PIECES):
+        arrive(beside, piece)
+        go(beside, piece, partner)
+        for step, way in hops:
+            origin = z - way * step
+            block = rail(origin, x)
+            here = inside(origin)
+            pl.when(here)(functools.partial(arrive, block, piece))
+            if step < depth - 1:
+                go(block, piece, rail(z + way, x), jnp.logical_and(here, inside(z + way)))
+            go(block, piece, beside, here)
+            go(block, piece, partner, here)
+        if piece > 0:
+            finish(piece - 1)
+
+            @pl.loop(0, width // cw)
+            def _(step):
+                cols = pl.ds(pl.multiple_of(step * cw, cw), cw)
+                if piece == 1:
+                    acc[:, cols] = product(0, cols)
+                else:
+                    acc[:, cols] += product(piece - 1, cols)
+
+    finish(PIECES - 1)
     every_id = rows[:, :, dim : dim + LANES].reshape(n * tok, LANES).astype(jnp.float32)
     lane = lax.broadcasted_iota(jnp.int32, (n * tok, LANES), 1).astype(jnp.float32)
     onehot = jnp.where(every_id == lane, 1.0, 0.0)
     onehot_t[...] = jnp.transpose(onehot)[0:clips].astype(jnp.bfloat16)
-    for load in loads[0]:
-        load.wait()
-    cw = 256
 
     @pl.loop(0, width // cw)
     def _(step):
         cols = pl.ds(pl.multiple_of(step * cw, cw), cw)
-        pre_act = jnp.dot(
-            rows[:, :, 0:dim].reshape(n * tok, dim), w1[:, cols], preferred_element_type=jnp.float32
-        )
+        pre_act = acc[:, cols] + product(PIECES - 1, cols)
         hidden = 0.5 * pre_act * (1.0 + lax.erf(pre_act * 0.7071067811865476))
         summed = jnp.dot(
             onehot_t[...], hidden.astype(jnp.bfloat16), preferred_element_type=jnp.float32
         )
         ph[:, cols] = (summed / FRAMES).astype(jnp.bfloat16)
 
-    for copy in sent:
-        copy.wait_send()
+    for copy, when in sent:
+        if when is True:
+            copy.wait_send()
+        else:
+            pl.when(when)(copy.wait_send)
     for load in loads[1]:
         load.wait()
     own_hot = jnp.where(
@@ -269,10 +357,11 @@
         functools.partial(kernel, n),
         name="vision_block",
         out_shape=jax.ShapeDtypeStruct((1, n * ew), bf16),
-        in_specs=[vmem, vmem, vmem, vmem, hbm, hbm, vmem, hbm],
+        in_specs=[vmem, vmem, vmem, hbm, hbm, vmem, hbm],
         out_specs=vmem,
         scratch_shapes=[
             pltpu.VMEM((n, tok, dim + LANES), bf16),
+            pltpu.VMEM((n * tok, width), f32),
             pltpu.VMEM((dim, width), bf16),
             pltpu.VMEM((width, dim), bf16),
             pltpu.VMEM((dim, ew), bf16),
@@ -284,8 +373,8 @@
             pltpu.VMEM((n, dim), bf16),
             pltpu.VMEM((n, 1, ew), f32),
             pltpu.VMEM((n, 1, ew), f32),
-            dma((3, 4)),
-            dma((n,)), dma((n,)), dma((n,)), dma((n,)),
+            dma((3, PIECES)),
+            dma((2 * n * PIECES,)), dma((n, PIECES)), dma((n,)), dma((n,)),
             dma((n,)), dma((n,)), dma((n,)), dma((n,)),
         ],
         compiler_params=pltpu.CompilerParams(
@@ -293,7 +382,6 @@
         ),
     )(
         frames_in,
-        jnp.broadcast_to(clip_ids[:, None], (tok, LANES)),
         clip_ids[None, :],
         norm_gain[None, :],
         expand_weight,

time: 69.6 us -> 59.5 us (0.85)
  Pallas kernels: 66.7 us -> 57.9 us
  local copies, waits for them, and re-layouts: 2.73 us -> 1.41 us
    pallas_call x1, Pallas kernels: 66.7 us -> 57.9 us  [fused(): pl.pallas_call(functools.partial(kernel, n), name='vision_block', out_sha...]
    broadcast_in_dim x1 -> x0, local copies, waits for them, and re-layouts: 1.32 us -> none  [fused(): jnp.broadcast_to(clip_ids[:, None], (tok, LANES))]
where the time goes in v3:
time: 59.5 us; the launch traced here: 59.3 us
  Pallas kernels  57.9 us (97%)
  local copies, waits for them, and re-layouts  1.41 us (2%)
    pallas_call x1, Pallas kernels, fused(): pl.pallas_call(functools.partial(kernel, n), name='vision_block', out_sha...  57.9 us
    unnamed x1, local copies, waits for them, and re-layouts  1.41 us

profile of v3, /device:TPU:0, one launch (start us, length us, event | category | flops | bytes accessed | tf_op | source)
XLA Modules:
  0.0 59.3 jit_solution(10992557988395170634)
XLA Ops:
  0.0 57.9 %vision_block.1 = bf16[1,8192]{1,0:T(2,128)(2,1)} custom-call(bf16[16,6144]{1,0:T(8,128)(2,1)} %frames_ref.1, s32[1,16]{1,0:T(1,128)} %bitcast.5, f32[1,6144]{1,0:T(1,128)} %bitcast.3, bf16[6144,1536]{1,0:T(8,128)(2,1)} %w1_hbm.1, bf16[1536,6144]{1,0:T(8,128)(2,1)} %w2_hbm.1, f32[1,6144]{1,0:T(1,128)} %bitcast.4, bf16[6144,512]{1,0:T(8,128)(2,1)} %w3_hbm.1), custom_call_target="tpu_custom_call" | custom-call | tf_op jit(solution)/shard_map/vision_block/pallas_call | solution.py:356
  57.9 1.4 %copy.9 = bf16[1,8192]{1,0:T(2,128)(2,1)} copy(bf16[1,8192]{1,0:T(2,128)(2,1)} %vision_block.1) | data formatting | bytes 32768

commit v4 on v3

--- a/solution.py
+++ b/solution.py
@@ -130,7 +130,8 @@
         for piece in range(PIECES):
             span = pl.ds(piece * tall, tall)
             load = pltpu.make_async_copy(src.at[span], dst.at[span], w_sem.at[index, piece])
-            load.start()
+            if index == 0:
+                load.start()
             group.append(load)
         loads.append(group)
 
@@ -192,7 +193,7 @@
             arrive(other * 2 + 1 - core, piece)
         loads[0][piece].wait()
 
-    cw = 256
+    cw = 512
 
     def product(piece, cols):
         span = slice(piece * deep, (piece + 1) * deep)
@@ -219,6 +220,9 @@
             go(block, piece, partner, here)
         if piece > 0:
             finish(piece - 1)
+            if piece == 1:
+                for load in loads[1] + loads[2]:
+                    load.start()
 
             @pl.loop(0, width // cw)
             def _(step):
@@ -396,7 +400,7 @@
     tok, dim = frames_in.shape
     width, ew = expand_weight.shape[1], conn_weight.shape[1]
     fits = tok == FRAMES and n % 16 == 0 and n <= LANES and (n * tok) % LANES == 0
-    even = dim % (n * LANES) == 0 and width % 256 == 0 and ew % LANES == 0
+    even = dim % (n * LANES) == 0 and width % 512 == 0 and ew % LANES == 0
     form = fused if fits and even else plain
     return form(
         frames_in, clip_ids, norm_gain, expand_weight, reduce_weight, conn_gain, conn_weight

time: 59.5 us -> 58.5 us (0.983)
  Pallas kernels: 57.9 us -> 56.9 us
    pallas_call x1, Pallas kernels: 57.9 us -> 56.9 us  [fused(): pl.pallas_call(functools.partial(kernel, n), name='vision_block', out_sha...]
where the time goes in v4:
time: 58.5 us; the launch traced here: 58.3 us
  Pallas kernels  56.9 us (97%)
  local copies, waits for them, and re-layouts  1.41 us (2%)
    pallas_call x1, Pallas kernels, fused(): pl.pallas_call(functools.partial(kernel, n), name='vision_block', out_sha...  56.9 us
    unnamed x1, local copies, waits for them, and re-layouts  1.41 us

profile of v4, /device:TPU:0, one launch (start us, length us, event | category | flops | bytes accessed | tf_op | source)
XLA Modules:
  0.0 58.3 jit_solution(15619789047299869560)
XLA Ops:
  0.0 56.9 %vision_block.1 = bf16[1,8192]{1,0:T(2,128)(2,1)} custom-call(bf16[16,6144]{1,0:T(8,128)(2,1)} %frames_ref.1, s32[1,16]{1,0:T(1,128)} %bitcast.5, f32[1,6144]{1,0:T(1,128)} %bitcast.3, bf16[6144,1536]{1,0:T(8,128)(2,1)} %w1_hbm.1, bf16[1536,6144]{1,0:T(8,128)(2,1)} %w2_hbm.1, f32[1,6144]{1,0:T(1,128)} %bitcast.4, bf16[6144,512]{1,0:T(8,128)(2,1)} %w3_hbm.1), custom_call_target="tpu_custom_call" | custom-call | tf_op jit(solution)/shard_map/vision_block/pallas_call | solution.py:360
  56.9 1.4 %copy.9 = bf16[1,8192]{1,0:T(2,128)(2,1)} copy(bf16[1,8192]{1,0:T(2,128)(2,1)} %vision_block.1) | data formatting | bytes 32768
